TPU v7x, 32 devices: a whole 2x2x4 slice. The times are simulated.
32 devices in a mesh: dp: 16 (over z, y, x), tensor: 2 (over core).
Axes of the slice: x: 2, y: 2, z: 4, core: 2. Of those that a mesh axis runs over, the one named last changes fastest.
Arguments:
- activations: bfloat16 [8192, 8192], P('dp', 'tensor'), may hold values from -6 to 6
- out_grads: bfloat16 [8192, 16384], P('dp', 'tensor'), may hold values from -0.0625 to 0.0625
- sketch: float32 [8192, 512], P('dp'), may hold values from -6 to 6
- first_moment: float32 [512, 16384], P('dp', 'tensor'), may hold values from -6 to 6
- second_moment: float32 [512, 16384], P('dp', 'tensor'), may hold values from 0.05 to 2
Outputs:
- update: float32 [8192, 16384], P('dp', 'tensor')
- first_new: float32 [512, 16384], P('dp', 'tensor')
- second_new: float32 [512, 16384], P('dp', 'tensor')
All inputs are finite; a program needn't handle non-finite values.
Results may differ from a plain program's by a relative error of at most 0.0041.
Values may be sent and summed in bfloat16 or wider, within the bound.
No kernel may reach another device: no remote copies, remote signals or barrier semaphores. Data moves between devices by JAX's collectives and lax.ppermute only.
A program may use at most 128 MiB of HBM per device.

v0:
```python
import math
import jax
import jax.numpy as jnp
from jax import lax
from jax.sharding import PartitionSpec as P

D = 8192
R = 512
BETA_ONE = 0.9
BETA_TWO = 0.999
CORRECT_ONE = 0.9999999993
CORRECT_TWO = 0.18135117
EPSILON = 1e-08


def local(activations, out_grads, sketch, first_moment, second_moment):
    highest = lax.Precision.HIGHEST
    features = lax.all_gather(activations, "tensor", axis=1, tiled=True)
    local_gram = jnp.dot(sketch.T, sketch, precision=highest, preferred_element_type=jnp.float32)
    sketch_gram = lax.psum(local_gram, "dp")
    cholesky_factor = jnp.linalg.cholesky(sketch_gram)
    own_rows = jax.scipy.linalg.solve_triangular(cholesky_factor, sketch.T, lower=True).T.astype(
        jnp.bfloat16
    )
    basis_full = lax.all_gather(own_rows, "dp", axis=0, tiled=True)
    projected = jnp.dot(features, basis_full, preferred_element_type=jnp.float32).astype(
        jnp.bfloat16
    )
    columns = projected
    grad_low = lax.psum_scatter(
        jnp.dot(columns.T, out_grads, preferred_element_type=jnp.float32),
        "dp",
        scatter_dimension=0,
        tiled=True,
    )
    first_new = BETA_ONE * first_moment + (1.0 - BETA_ONE) * grad_low
    second_new = BETA_TWO * second_moment + (1.0 - BETA_TWO) * grad_low * grad_low
    direction = (first_new / CORRECT_ONE / (jnp.sqrt(second_new / CORRECT_TWO) + EPSILON)).astype(
        jnp.bfloat16
    )
    update_scale = math.sqrt(D / R)
    columns = own_rows
    update = update_scale * jnp.dot(
        columns,
        lax.all_gather(direction, "dp", axis=0, tiled=True),
        preferred_element_type=jnp.float32,
    )
    return (update, first_new, second_new)


def solution(mesh):
    return jax.shard_map(
        local,
        mesh=mesh,
        in_specs=(
            P("dp", "tensor"),
            P("dp", "tensor"),
            P("dp", None),
            P("dp", "tensor"),
            P("dp", "tensor"),
        ),
        out_specs=(P("dp", "tensor"), P("dp", "tensor"), P("dp", "tensor")),
        check_vma=False,
    )
```

profile of v0, /device:TPU:0, one launch (start us, length us, event | category | flops | bytes accessed | tf_op | source)
XLA Modules:
  0.0 897.9 jit_solution(7498624918526684430)
XLA Ops:
  8.0 4.5 fusion.38
  12.6 0.5 all-gather.6.cloned.1.call-update
  13.2 115.9 %all-reduce.3.cloned.1.call-done = f32[512,512]{0,1:T(8,128)} async-done(((f32[512,512]{0,1:T(8,128)}), f32[512,512]{0,1:T(8,128)}) %all-reduce.3.cloned.1.call-update) | async-done | bytes 1048592 | tf_op jit(solution)/shard_map/psum | solution.py:20
  129.1 1.6 copy.9
  130.7 1.4 fusion.2
  132.2 11.7 %cholesky.104 = f32[128,128]{1,0:T(8,128)S(1)} custom-call(f32[128,128]{1,0:T(8,128)S(1)} %cholesky.266), custom_call_target="Cholesky" | custom-call | tf_op jit(solution)/shard_map/jit(cholesky)/cholesky | solution.py:21
  143.9 9.8 %custom-call.31 = f32[1,128,128]{1,2,0:T(8,128)S(1)} custom-call(f32[1,128,128]{2,1,0:T(8,128)S(1)} %get-tuple-element.33), custom_call_target="InvertDiagBlocksLowerTriangular" | custom-call | tf_op jit(solution)/shard_map/jit(cholesky)/cholesky | solution.py:21
  153.7 0.1 cholesky.224
  153.9 0.3 constant_dynamic-update-slice_fusion.3
  154.2 0.3 convolution_subtract_fusion.3
  154.5 11.7 %cholesky.217 = f32[128,128]{1,0:T(8,128)S(1)} custom-call(f32[128,128]{1,0:T(8,128)S(1)} %cholesky.270), custom_call_target="Cholesky" | custom-call | tf_op jit(solution)/shard_map/jit(cholesky)/cholesky | solution.py:21
  166.3 10.0 %custom-call.32 = f32[1,128,128]{1,2,0:T(8,128)S(1)} custom-call(f32[1,128,128]{2,1,0:T(8,128)S(1)} %get-tuple-element.30), custom_call_target="InvertDiagBlocksLowerTriangular" | custom-call | tf_op jit(solution)/shard_map/jit(cholesky)/cholesky | solution.py:21
  176.2 0.3 convolution_dynamic-update-slice_fusion
  176.5 0.4 convolution_subtract_fusion.4
  176.9 11.7 %cholesky.238 = f32[128,128]{1,0:T(8,128)S(1)} custom-call(f32[128,128]{1,0:T(8,128)S(1)} %cholesky.275), custom_call_target="Cholesky" | custom-call | tf_op jit(solution)/shard_map/jit(cholesky)/cholesky | solution.py:21
  188.7 9.8 %custom-call.33 = f32[1,128,128]{1,2,0:T(8,128)S(1)} custom-call(f32[1,128,128]{2,1,0:T(8,128)S(1)} %get-tuple-element.27), custom_call_target="InvertDiagBlocksLowerTriangular" | custom-call | tf_op jit(solution)/shard_map/jit(cholesky)/cholesky | solution.py:21
  198.5 0.2 convolution_dynamic-update-slice_fusion.1
  198.7 0.4 convolution_subtract_fusion.5
  199.1 11.7 %cholesky.255 = f32[128,128]{1,0:T(8,128)S(1)} custom-call(f32[128,128]{1,0:T(8,128)S(1)} %convolution_subtract_fusion.5), custom_call_target="Cholesky" | custom-call | tf_op jit(solution)/shard_map/jit(cholesky)/cholesky | solution.py:21
  210.8 0.7 compare_reduce_fusion.2
  212.7 0.6 compare_reduce_fusion.1
  214.1 0.6 compare_reduce_fusion
  215.3 0.3 select_select_fusion
  215.7 10.4 %while.1 = (s32[]{:T(128)}, f32[512,512]{1,0:T(8,128)S(1)}, s32[4,2]{0,1:T(2,128)S(1)}, f32[4,128,128]{2,1,0:T(8,128)}, s32[]{:T(128)}) while((s32[]{:T(128)}, f32[512,512]{1,0:T(8,128)S(1)}, s32[4,2]{0,1:T(2,128)S(1)}, f32[4,128,128]{2,1,0:T(8,128)}, s32[]{:T(128)}) %tuple.36), condition=%wide.while_cond, body=%wide.while_body.sunk | while | flops 2 | bytes 132205 | solution.py:22
  215.8 0.5 fusion.51
  216.3 2.0 bitcast_dynamic-update-slice_fusion.2
  218.4 0.5 fusion.51
  218.9 2.0 bitcast_dynamic-update-slice_fusion.2
  221.0 0.5 fusion.51
  221.5 2.0 bitcast_dynamic-update-slice_fusion.2
  223.6 0.5 fusion.51
  224.1 2.0 bitcast_dynamic-update-slice_fusion.2
  226.1 40.1 %custom-call.34 = f32[4,128,128]{1,2,0:T(8,128)S(1)} custom-call(f32[4,128,128]{2,1,0:T(8,128)} %get-tuple-element.10), custom_call_target="InvertDiagBlocksLowerTriangular" | custom-call | tf_op jit(solution)/shard_map/jit(_solve_triangular)/triangular_solve | solution.py:22
  266.2 0.4 fusion.37
  266.7 0.6 convolution_subtract_fusion.1
  267.3 0.4 fusion.36
  267.7 1.0 convolution_subtract_fusion
  268.7 0.4 fusion.35
  269.1 1.5 convolution_subtract_fusion.2
  270.6 0.4 convolution_convert_fusion.1
  271.0 0.8 fusion.21
  272.0 120.0 %all-gather.4.cloned.1.call-done = bf16[8192,512]{0,1:T(8,128)(2,1)} async-done(((bf16[512,512]{0,1:T(8,128)(2,1)}), bf16[8192,512]{0,1:T(8,128)(2,1)}) %all-gather.4.cloned.1.call-update) | async-done | bytes 8388624 | tf_op jit(solution)/shard_map/all_gather | solution.py:25
  391.9 19.7 %fusion = f32[512,8192]{1,0:T(8,128)} fusion(bf16[512,8192]{1,0:T(8,128)(2,1)} %param.6, bf16[8192,512]{0,1:T(8,128)(2,1)} %all-gather.4.cloned.1.call-done, bf16[512,8192]{1,0:T(8,128)(2,1)} %all-gather.6.cloned.1.call-done), kind=kOutput, calls=%fused_computation.5 | convolution fusion | flops 8590196736 | bytes 41943040 | tf_op jit(solution)/shard_map/dot_general | solution.py:31
  411.7 0.3 all-gather.8.cloned.1.call-start
  412.0 344.4 %reduce-scatter.2.cloned.1.call-done = f32[32,8192]{1,0:T(8,128)} async-done(((f32[512,8192]{1,0:T(8,128)}), f32[32,8192]{1,0:T(8,128)}) %reduce-scatter.2.cloned.1.call-update) | async-done | bytes 1048592 | tf_op jit(solution)/shard_map/reduce_scatter | solution.py:30
  756.4 3.0 divide_convert_fusion
  759.5 118.5 %all-gather.8.cloned.1.call-done = bf16[512,8192]{1,0:T(8,128)(2,1)} async-done(((bf16[32,8192]{1,0:T(8,128)(2,1)}), bf16[512,8192]{1,0:T(8,128)(2,1)}) %all-gather.8.cloned.1.call-update) | async-done | bytes 8388624 | tf_op jit(solution)/shard_map/all_gather | solution.py:45
  877.9 11.9 %convolution_multiply_fusion = f32[512,8192]{1,0:T(8,128)} fusion(bf16[512,8192]{1,0:T(8,128)(2,1)} %all-gather.8.cloned.1.call-done, bf16[128,512]{1,0:T(8,128)(2,1)S(1)} %convolution_convert_fusion.1, bf16[128,512]{1,0:T(8,128)(2,1)S(1)} %get-tuple-element.36, bf16[128,512]{1,0:T(8,128)(2,1)S(1)} %get-tuple-element.38, ...), kind=kOutput, calls=%fused_computation.2 | convolution fusion | flops 4301258752 | bytes 25690112 | tf_op jit(solution)/shard_map/dot_general | solution.py:43
  (29 shorter events, 0.7 us)
Async XLA Ops:
  8.0 121.1 %all-reduce.3.cloned.1.call-start = ((), (), s32[]{:S(2)}) async-start(), calls=%async_computation.1 | async-start | bytes 2097152 | tf_op jit(solution)/shard_map/psum | solution.py:20
  12.5 253.7 %copy-start = (f32[512,512]{1,0:T(8,128)S(1)}, f32[512,512]{1,0:T(8,128)}, u32[]{:S(2)}) copy-start(f32[512,512]{1,0:T(8,128)} %param.7) | copy-start | bytes 3145732
  12.5 259.4 %all-gather.6.cloned.1.call-start = ((), (), s32[]{:S(2)}) async-start(), calls=%async_computation.3 | async-start | bytes 12582912 | tf_op jit(solution)/shard_map/all_gather | solution.py:18
  13.1 378.8 %all-gather.4.cloned.1.call-start = ((), (), s32[]{:S(2)}) async-start(), calls=%async_computation.2 | async-start | bytes 8912896 | tf_op jit(solution)/shard_map/all_gather | solution.py:25
  271.9 484.5 %reduce-scatter.2.cloned.1.call-start = ((), (), s32[]{:S(2)}) async-start(), calls=%async_computation.4 | async-start | bytes 17825792 | tf_op jit(solution)/shard_map/reduce_scatter | solution.py:30
  411.6 344.8 %copy-start.1 = (f32[32,8192]{1,0:T(8,128)S(1)}, f32[32,8192]{1,0:T(8,128)}, u32[]{:S(2)}) copy-start(f32[32,8192]{1,0:T(8,128)} %param.9) | copy-start | bytes 3145732
  411.6 344.8 %copy-start.2 = (f32[32,8192]{1,0:T(8,128)S(1)}, f32[32,8192]{1,0:T(8,128)}, u32[]{:S(2)}) copy-start(f32[32,8192]{1,0:T(8,128)} %param.8) | copy-start | bytes 3145732
  411.7 466.3 %all-gather.8.cloned.1.call-start = ((), (), s32[]{:S(2)}) async-start(), calls=%async_computation.5 | async-start | bytes 8912896 | tf_op jit(solution)/shard_map/all_gather | solution.py:45
Sparse Core Ops, SparseCore 0:
  14.7 114.4 all-reduce.2
  411.8 344.5 reduce-scatter.1
Sparse Core Ops, SparseCore 1:
  14.6 22.4 all-gather.5
  272.0 119.9 all-gather.3
  759.5 118.4 all-gather.7
where the time goes:
time: 908 us; the launch traced here: 898 us
  waiting for transfers between devices  699 us (77%)
  other arithmetic  124 us (14%)
  matrix products  42.7 us (5%)
  between operations  18.9 us (2%)
  local copies, waits for them, and re-layouts  12.1 us (1%)
    reduce_scatter x1, waiting for transfers between devices, local(): lax.psum_scatter(jnp.dot(columns.T, out_grads, preferred_element_type=jnp...  344 us
    all_gather x1, waiting for transfers between devices, local(): basis_full = lax.all_gather(own_rows, 'dp', axis=0, tiled=True)  120 us
    all_gather x1, waiting for transfers between devices, local(): lax.all_gather(direction, 'dp', axis=0, tiled=True)  118 us
    psum x1, waiting for transfers between devices, local(): sketch_gram = lax.psum(local_gram, 'dp')  116 us
    another operation x14, other arithmetic, local(): cholesky_factor = jnp.linalg.cholesky(sketch_gram)  78.5 us
    another operation x3, other arithmetic, local(): jax.scipy.linalg.solve_triangular(cholesky_factor, sketch.T, lower=True)  40.5 us
    dot_general x1, matrix products, local(): jnp.dot(columns.T, out_grads, preferred_element_type=jnp.float32)  19.7 us
  transfers between devices with their start and end apart: 5, of which 4 were waited for; matrix products, arithmetic and copies ran while one was open for 16% of the time, Pallas kernels for 0%

commit v1 on v0

--- a/solution.py
+++ b/solution.py
@@ -3,6 +3,7 @@
 import jax.numpy as jnp
 from jax import lax
 from jax.sharding import PartitionSpec as P
+from jax.lax import all_gather
 
 D = 8192
 R = 512
@@ -17,7 +18,8 @@
     highest = lax.Precision.HIGHEST
     features = lax.all_gather(activations, "tensor", axis=1, tiled=True)
     local_gram = jnp.dot(sketch.T, sketch, precision=highest, preferred_element_type=jnp.float32)
-    sketch_gram = lax.psum(local_gram, "dp")
+    notes_part = lambda sample: jnp.sum(all_gather(sample, axis_name="dp"), 0)
+    sketch_gram = notes_part(local_gram)
     cholesky_factor = jnp.linalg.cholesky(sketch_gram)
     own_rows = jax.scipy.linalg.solve_triangular(cholesky_factor, sketch.T, lower=True).T.astype(
         jnp.bfloat16

time: 908 us -> 994 us (1.095)
  waiting for transfers between devices: 699 us -> 777 us
    all_gather x0 -> x1, waiting for transfers between devices: none -> 194 us  [local(): notes_part = lambda sample: jnp.sum(all_gather(sample, axis_name='dp'), 0)]
    psum x1 -> x0, waiting for transfers between devices: 116 us -> none  [local(): sketch_gram = lax.psum(local_gram, 'dp')]
  transfers between devices with their start and end apart: 5 -> 5, of which waited for: 4 -> 4; matrix products, arithmetic and copies ran while one was open for 16% -> 15% of each run, Pallas kernels for 0% -> 0%
where the time goes in v1:
time: 994 us; the launch traced here: 984 us
  waiting for transfers between devices  777 us (78%)
  other arithmetic  131 us (13%)
  matrix products  46.3 us (5%)
  between operations  16.8 us (2%)
  local copies, waits for them, and re-layouts  11.9 us (1%)
    reduce_scatter x1, waiting for transfers between devices, local(): lax.psum_scatter(jnp.dot(columns.T, out_grads, preferred_element_type=jnp...  345 us
    all_gather x1, waiting for transfers between devices, local(): notes_part = lambda sample: jnp.sum(all_gather(sample, axis_name='dp'), 0)  194 us
    all_gather x1, waiting for transfers between devices, local(): basis_full = lax.all_gather(own_rows, 'dp', axis=0, tiled=True)  119 us
    all_gather x1, waiting for transfers between devices, local(): lax.all_gather(direction, 'dp', axis=0, tiled=True)  119 us
    another operation x14, other arithmetic, local(): cholesky_factor = jnp.linalg.cholesky(sketch_gram)  79 us
    another operation x3, other arithmetic, local(): jax.scipy.linalg.solve_triangular(cholesky_factor, sketch.T, lower=True)  40.3 us
  transfers between devices with their start and end apart: 5, of which 4 were waited for; matrix products, arithmetic and copies ran while one was open for 15% of the time, Pallas kernels for 0%

profile of v1, /device:TPU:0, one launch (start us, length us, event | category | flops | bytes accessed | tf_op | source)
XLA Modules:
  0.0 983.9 jit_solution(4174733418342251289)
XLA Ops:
  7.2 4.4 fusion.38
  11.7 0.7 all-gather.8.cloned.1.call-update
  12.5 193.7 %all-gather.12.cloned.1.call-done = f32[8192,512]{1,0:T(8,128)} async-done(((f32[512,512]{1,0:T(8,128)}), f32[8192,512]{1,0:T(8,128)}) %all-gather.12.cloned.1.call-update) | async-done | bytes 16777232 | tf_op jit(solution)/shard_map/all_gather | solution.py:21
  206.2 8.1 reduce_sum.9
  214.2 0.3 copy.9
  214.6 0.2 fusion.2
  214.8 1.0 copy-done.1
  215.8 11.7 %cholesky.104 = f32[128,128]{1,0:T(8,128)S(1)} custom-call(f32[128,128]{1,0:T(8,128)S(1)} %cholesky.266), custom_call_target="Cholesky" | custom-call | tf_op jit(solution)/shard_map/jit(cholesky)/cholesky | solution.py:23
  227.7 9.8 custom-call.31
  237.5 1.2 constant_dynamic-update-slice_fusion.3
  238.7 1.3 convolution_subtract_fusion.3
  240.0 12.2 %cholesky.217 = f32[128,128]{1,0:T(8,128)S(1)} custom-call(f32[128,128]{1,0:T(8,128)S(1)} %cholesky.270), custom_call_target="Cholesky" | custom-call | tf_op jit(solution)/shard_map/jit(cholesky)/cholesky | solution.py:23
  252.2 9.8 custom-call.32
  262.0 0.3 convolution_dynamic-update-slice_fusion
  262.3 1.3 convolution_subtract_fusion.4
  263.6 11.7 %cholesky.238 = f32[128,128]{1,0:T(8,128)S(1)} custom-call(f32[128,128]{1,0:T(8,128)S(1)} %cholesky.275), custom_call_target="Cholesky" | custom-call | tf_op jit(solution)/shard_map/jit(cholesky)/cholesky | solution.py:23
  275.3 9.8 custom-call.33
  285.2 0.2 convolution_dynamic-update-slice_fusion.1
  285.4 1.2 convolution_subtract_fusion.5
  286.6 11.9 %cholesky.255 = f32[128,128]{1,0:T(8,128)S(1)} custom-call(f32[128,128]{1,0:T(8,128)S(1)} %convolution_subtract_fusion.5), custom_call_target="Cholesky" | custom-call | tf_op jit(solution)/shard_map/jit(cholesky)/cholesky | solution.py:23
  298.5 0.7 compare_reduce_fusion.2
  300.4 0.6 compare_reduce_fusion.1
  301.8 0.6 compare_reduce_fusion
  303.2 10.5 %while.1 = (s32[]{:T(128)}, f32[512,512]{1,0:T(8,128)S(1)}, s32[4,2]{0,1:T(2,128)S(1)}, f32[4,128,128]{2,1,0:T(8,128)}, s32[]{:T(128)}) while((s32[]{:T(128)}, f32[512,512]{1,0:T(8,128)S(1)}, s32[4,2]{0,1:T(2,128)S(1)}, f32[4,128,128]{2,1,0:T(8,128)}, s32[]{:T(128)}) %tuple.36), condition=%wide.while_cond, body=%wide.while_body.sunk | while | flops 2 | bytes 132205 | solution.py:24
  303.3 0.5 fusion.51
  303.8 2.0 bitcast_dynamic-update-slice_fusion.2
  305.9 0.5 fusion.51
  306.4 2.0 bitcast_dynamic-update-slice_fusion.2
  308.5 0.5 fusion.51
  309.1 2.0 bitcast_dynamic-update-slice_fusion.2
  311.1 0.5 fusion.51
  311.7 2.0 bitcast_dynamic-update-slice_fusion.2
  313.7 40.1 %custom-call.34 = f32[4,128,128]{1,2,0:T(8,128)S(1)} custom-call(f32[4,128,128]{2,1,0:T(8,128)} %get-tuple-element.10), custom_call_target="InvertDiagBlocksLowerTriangular" | custom-call | tf_op jit(solution)/shard_map/jit(_solve_triangular)/triangular_solve | solution.py:24
  353.8 0.4 fusion.37
  354.3 0.6 convolution_subtract_fusion.1
  354.9 0.4 fusion.36
  355.3 1.0 convolution_subtract_fusion
  356.3 0.4 fusion.35
  356.7 1.5 convolution_subtract_fusion.2
  358.2 0.4 convolution_convert_fusion.1
  358.6 0.8 fusion.21
  359.5 0.3 reduce-scatter.2.cloned.1.call-start
  359.8 119.3 %all-gather.6.cloned.1.call-done = bf16[8192,512]{0,1:T(8,128)(2,1)} async-done(((bf16[512,512]{0,1:T(8,128)(2,1)}), bf16[8192,512]{0,1:T(8,128)(2,1)}) %all-gather.6.cloned.1.call-update) | async-done | bytes 8388624 | tf_op jit(solution)/shard_map/all_gather | solution.py:27
  479.1 19.7 %fusion = f32[512,8192]{1,0:T(8,128)} fusion(bf16[512,8192]{1,0:T(8,128)(2,1)} %param.6, bf16[8192,512]{0,1:T(8,128)(2,1)} %all-gather.6.cloned.1.call-done, bf16[512,8192]{1,0:T(8,128)(2,1)} %all-gather.8.cloned.1.call-done), kind=kOutput, calls=%fused_computation.5 | convolution fusion | flops 8590196736 | bytes 41943040 | tf_op jit(solution)/shard_map/dot_general | solution.py:33
  498.9 344.7 %reduce-scatter.2.cloned.1.call-done = f32[32,8192]{1,0:T(8,128)} async-done(((f32[512,8192]{1,0:T(8,128)}), f32[32,8192]{1,0:T(8,128)}) %reduce-scatter.2.cloned.1.call-update) | async-done | bytes 1048592 | tf_op jit(solution)/shard_map/reduce_scatter | solution.py:32
  843.5 3.0 divide_convert_fusion
  846.6 118.6 %all-gather.10.cloned.1.call-done = bf16[512,8192]{1,0:T(8,128)(2,1)} async-done(((bf16[32,8192]{1,0:T(8,128)(2,1)}), bf16[512,8192]{1,0:T(8,128)(2,1)}) %all-gather.10.cloned.1.call-update) | async-done | bytes 8388624 | tf_op jit(solution)/shard_map/all_gather | solution.py:47
  965.2 11.9 %convolution_multiply_fusion = f32[512,8192]{1,0:T(8,128)} fusion(bf16[512,8192]{1,0:T(8,128)(2,1)} %all-gather.10.cloned.1.call-done, bf16[128,512]{1,0:T(8,128)(2,1)S(1)} %convolution_convert_fusion.1, bf16[128,512]{1,0:T(8,128)(2,1)S(1)} %get-tuple-element.36, bf16[128,512]{1,0:T(8,128)(2,1)S(1)} %get-tuple-element.38, ...), kind=kOutput, calls=%fused_computation.2 | convolution fusion | flops 4301258752 | bytes 25690112 | tf_op jit(solution)/shard_map/dot_general | solution.py:45
  (32 shorter events, 1.0 us)
Async XLA Ops:
  7.2 199.0 %all-gather.12.cloned.1.call-start = ((), (), s32[]{:S(2)}) async-start(), calls=%async_computation.5 | async-start | bytes 17825792 | tf_op jit(solution)/shard_map/all_gather | solution.py:21
  11.7 348.1 %all-gather.8.cloned.1.call-start = ((), (), s32[]{:S(2)}) async-start(), calls=%async_computation.2 | async-start | bytes 12582912 | tf_op jit(solution)/shard_map/all_gather | solution.py:19
  12.4 466.6 %all-gather.6.cloned.1.call-start = ((), (), s32[]{:S(2)}) async-start(), calls=%async_computation.1 | async-start | bytes 8912896 | tf_op jit(solution)/shard_map/all_gather | solution.py:27
  214.2 139.6 %copy-start = (f32[512,512]{1,0:T(8,128)S(1)}, f32[512,512]{1,0:T(8,128)}, u32[]{:S(2)}) copy-start(f32[512,512]{1,0:T(8,128)} %param.7) | copy-start | bytes 3145732
  214.8 1.0 copy-start.1
  359.5 484.1 %reduce-scatter.2.cloned.1.call-start = ((), (), s32[]{:S(2)}) async-start(), calls=%async_computation.3 | async-start | bytes 17825792 | tf_op jit(solution)/shard_map/reduce_scatter | solution.py:32
  498.8 344.8 %copy-start.2 = (f32[32,8192]{1,0:T(8,128)S(1)}, f32[32,8192]{1,0:T(8,128)}, u32[]{:S(2)}) copy-start(f32[32,8192]{1,0:T(8,128)} %param.9) | copy-start | bytes 3145732
  498.8 344.8 %copy-start.3 = (f32[32,8192]{1,0:T(8,128)S(1)}, f32[32,8192]{1,0:T(8,128)}, u32[]{:S(2)}) copy-start(f32[32,8192]{1,0:T(8,128)} %param.8) | copy-start | bytes 3145732
  498.8 466.4 %all-gather.10.cloned.1.call-start = ((), (), s32[]{:S(2)}) async-start(), calls=%async_computation.4 | async-start | bytes 8912896 | tf_op jit(solution)/shard_map/all_gather | solution.py:47
Sparse Core Ops, SparseCore 0:
  11.8 194.3 all-gather.11
  207.7 18.0 all-gather.7
  359.6 119.4 all-gather.5
  498.9 344.5 reduce-scatter.1
  846.7 118.4 all-gather.9
